TPU v7x, 32 devices: a whole 2x2x4 slice. The times are simulated.
32 devices in a mesh: groups: 2 (over x), dp: 2 (over core), tensor: 8 (over z, y).
Axes of the slice: x: 2, y: 2, z: 4, core: 2. Of those that a mesh axis runs over, the one named last changes fastest.
Arguments:
- hidden: bfloat16 [4, 1024, 8192], P(('groups', 'dp'), 'tensor'), parts along dimension 0, may hold values from -24 to 24
- query_weight: bfloat16 [8192, 4096], P(None, 'tensor'), may hold values from -0.0625 to 0.0625
- key_weight: bfloat16 [8, 4096, 128], P('tensor'), may hold values from -0.0625 to 0.0625
- value_weight: bfloat16 [8, 4096, 128], P('tensor'), may hold values from -0.0625 to 0.0625
- head_grad: bfloat16 [4, 1024, 4096], P(('groups', 'dp'), None, 'tensor'), parts along dimension 0, may hold values from -6 to 6
- lengths: int32 [4], P(('groups', 'dp')), parts along dimension 0, may hold values from 256 to 1024, as said below
Outputs:
- fisher_key: float32 [16, 4096, 128], P(('groups', 'tensor'), 'dp'), parts along dimension 0
- fisher_value: float32 [16, 4096, 128], P(('groups', 'tensor'), 'dp'), parts along dimension 0
There are 2 independent parts, one for each index of `groups`. A program takes and returns all parts, laid end to end along the dimension named above; an argument that names none is the same for every part. Nothing has to cross between parts.
Inputs may be any that keep to these rules, and one draw needn't show every extreme that they name: `lengths`: some sequence of each part has length 1024.
All inputs are finite; a program needn't handle non-finite values.
Results may differ from a plain program's by a relative error of at most 0.013.
The roundings to bfloat16 on the way count: a program that leaves them out, or rounds other values in their place, can miss the bound.
Values may be sent and summed in bfloat16 or wider, within the bound.
A program may use at most 256 MiB of HBM per device.

v0:
```python
import math
import jax
import jax.numpy as jnp
from jax import lax
from jax.sharding import PartitionSpec as P

rope_base = 1000000.0
far_below = -1e30


def from_partner(value, axis, stride):
    mask = 2**stride
    pairs = [(source, source ^ mask) for source in range(lax.axis_size(axis))]
    return lax.ppermute(value, axis, pairs)


def angle_table(length, head_width):
    position = jnp.arange(length, dtype=jnp.float32)[:, None]
    frequency = rope_base ** (-2.0 * jnp.arange(head_width // 2, dtype=jnp.float32) / head_width)
    return (position * frequency)[:, None, :]


def rotate(vectors, angles):
    half_dim = vectors.shape[-1] // 2
    lead_half = vectors[..., :half_dim]
    tail_half = vectors[..., half_dim:]
    cosine = jnp.cos(angles)
    sines = jnp.sin(angles)
    return jnp.concatenate(
        [lead_half * cosine - tail_half * sines, tail_half * cosine + lead_half * sines], axis=-1
    )


def unrotate(vectors, angles):
    half_dim = vectors.shape[-1] // 2
    lead_half = vectors[..., :half_dim]
    tail_half = vectors[..., half_dim:]
    cosine = jnp.cos(angles)
    sines = jnp.sin(angles)
    return jnp.concatenate(
        [lead_half * cosine + tail_half * sines, tail_half * cosine - lead_half * sines], axis=-1
    )


def local(hidden, query_weight, key_weight, value_weight, head_grad, lengths):
    seq_count, tok_rows, model_width = hidden.shape
    length = tok_rows * lax.axis_size("tensor")
    half_width = model_width // 2
    head_width = key_weight.shape[2]
    heads_here = query_weight.shape[1] // head_width
    query_cols = heads_here * head_width
    pair_side = lax.axis_index("tensor") % 2
    score_scale = 1.0 / math.sqrt(head_width)
    angles = angle_table(length, head_width)
    pair_rows = jnp.concatenate([key_weight[0], value_weight[0]], axis=1)
    collected_rows = lax.all_gather(hidden, "tensor", axis=1, tiled=True)
    query_part = jnp.dot(collected_rows, query_weight, preferred_element_type=jnp.float32)
    own_part = lax.dynamic_slice_in_dim(collected_rows, pair_side * half_width, half_width, 2)
    kv_part = jnp.dot(own_part, pair_rows, preferred_element_type=jnp.float32)
    projected = jnp.concatenate([query_part, kv_part], axis=-1)
    kv_mixed = projected[..., query_cols:]
    kv_mixed = kv_mixed + from_partner(kv_mixed, "tensor", 0)
    queries = rotate(
        projected[..., :query_cols].reshape(seq_count, length, heads_here, head_width), angles
    ).astype(jnp.bfloat16)
    keys = rotate(kv_mixed[..., :head_width][:, :, None, :], angles)[:, :, 0, :].astype(
        jnp.bfloat16
    )
    values = kv_mixed[..., head_width:].astype(jnp.bfloat16)
    live_rows = jnp.arange(length, dtype=jnp.int32)[None, :] < lengths[:, None]
    upstream = jnp.where(live_rows[:, :, None], head_grad, jnp.zeros_like(head_grad)).reshape(
        seq_count, length, heads_here, head_width
    )
    block_rows = 512
    block_count = length // block_rows
    kv_accum = jnp.zeros((seq_count, length, 2 * head_width), jnp.float32)
    for block_idx in range(block_count):
        row_begin = block_idx * block_rows
        row_end = row_begin + block_rows
        query_block = queries[:, row_begin:row_end]
        up_block = upstream[:, row_begin:row_end]
        key_tile_block = keys[:, :row_end]
        value_block = values[:, :row_end]
        scores = (
            jnp.einsum(
                "sqhd,skd->shqk", query_block, key_tile_block, preferred_element_type=jnp.float32
            )
            * score_scale
        )
        causal_ok = (row_begin + jnp.arange(block_rows))[:, None] >= jnp.arange(row_end)[None, :]
        scores = jnp.where(causal_ok, scores, far_below)
        exp_scores = jnp.exp(scores - jnp.max(scores, axis=-1, keepdims=True))
        prob_rows = exp_scores / jnp.sum(exp_scores, axis=-1, keepdims=True)
        dprob = jnp.einsum(
            "sqhd,skd->shqk", up_block, value_block, preferred_element_type=jnp.float32
        )
        row_dot = jnp.sum(prob_rows * dprob, axis=-1, keepdims=True)
        dscore = (prob_rows * (dprob - row_dot) * score_scale).astype(jnp.bfloat16)
        key_portion = jnp.einsum(
            "shqk,sqhd->skd", dscore, query_block, preferred_element_type=jnp.float32
        )
        value_part = jnp.einsum(
            "shqk,sqhd->skd",
            prob_rows.astype(jnp.bfloat16),
            up_block,
            preferred_element_type=jnp.float32,
        )
        block_grad = jnp.concatenate([key_portion, value_part], axis=-1)
        kv_accum = kv_accum + jnp.pad(block_grad, ((0, 0), (0, length - row_end), (0, 0)))
    kv_accum = kv_accum + from_partner(kv_accum, "tensor", 0)
    key_gradient = unrotate(kv_accum[..., :head_width][:, :, None, :], angles)[:, :, 0, :]
    key_value_gradient = jnp.concatenate(
        [key_gradient, kv_accum[..., head_width:]], axis=-1
    ).astype(jnp.bfloat16)
    owned_columns = lax.dynamic_slice_in_dim(collected_rows, pair_side * half_width, half_width, 2)
    sample_count = jnp.einsum(
        "jyv,jyo->jvo", owned_columns, key_value_gradient, preferred_element_type=jnp.float32
    )
    squares = jnp.sum(sample_count * sample_count, axis=0)
    fisher_key, fisher_value = (
        lax.psum_scatter(squares[:, :head_width], "dp", scatter_dimension=0, tiled=True),
        lax.psum_scatter(squares[:, head_width:], "dp", scatter_dimension=0, tiled=True),
    )
    return (fisher_key[None], fisher_value[None])


def solution(mesh):
    in_specs = (
        P(("groups", "dp"), "tensor", None),
        P(None, "tensor"),
        P("tensor", None, None),
        P("tensor", None, None),
        P(("groups", "dp"), None, "tensor"),
        P(("groups", "dp")),
    )
    out_specs = (P(("groups", "tensor"), "dp", None), P(("groups", "tensor"), "dp", None))
    return jax.shard_map(local, mesh=mesh, in_specs=in_specs, out_specs=out_specs, check_vma=False)
```

profile of v0, /device:TPU:0, one launch (start us, length us, event | category | flops | bytes accessed | tf_op | source)
XLA Modules:
  0.0 360.1 jit_solution(1559386330099793040)
XLA Ops:
  7.2 0.7 all-gather.2.cloned.1.call-update
  8.0 11.4 %copy.50 = bf16[512,8192]{1,0:T(8,128)(2,1)} copy(bf16[512,8192]{0,1:T(8,128)(2,1)} %bitcast.207) | data formatting | bytes 16777216 | tf_op jit(solution)/shard_map/dot_general | solution.py:57
  19.3 0.5 copy.24
  20.7 1.0 fusion.80
  21.7 0.4 iota_compare_fusion
  22.1 218.3 %all-gather.2.cloned.1.call-done = bf16[1,1024,8192]{2,1,0:T(8,128)(2,1)} async-done(((bf16[1,128,8192]{2,1,0:T(8,128)(2,1)}), bf16[1,1024,8192]{2,1,0:T(8,128)(2,1)}) %all-gather.2.cloned.1.call-update) | async-done | bytes 16777232 | tf_op jit(solution)/shard_map/all_gather | solution.py:56
  240.5 6.3 %fusion.49 = f32[1,1024,256]{1,2,0:T(8,128)S(1)} fusion(bf16[4096,128]{1,0:T(8,128)(2,1)} %bitcast.215, bf16[4096,128]{1,0:T(8,128)(2,1)} %bitcast.216, bf16[1,1024,8192]{2,1,0:T(8,128)(2,1)} %all-gather.2.cloned.1.call-done, s32[]{:T(128)S(6)} %select_n.24), kind=kOutput, calls=%fused_computation.48 | convolution fusion | flops 2151677952 | bytes 11534340 | tf_op jit(solution)/shard_map/dot_general | solution.py:59
  246.8 0.6 collective-permute-start
  247.4 14.4 %fusion.44 = f32[1,1024,4,128]{1,3,2,0:T(8,128)S(1)} fusion(bf16[4,128,8192]{2,1,0:T(8,128)(2,1)} %bitcast.208, bf16[1,1024,8192]{2,1,0:T(8,128)(2,1)} %all-gather.2.cloned.1.call-done), kind=kOutput, calls=%fused_computation.47 | convolution fusion | flops 8589934592 | bytes 27262976 | tf_op jit(solution)/shard_map/dot_general | solution.py:57
  261.8 0.4 add_convert_fusion
  262.1 9.2 %collective-permute-done = f32[1,1024,256]{1,2,0:T(8,128)S(1)} collective-permute-done((f32[1,1024,256]{1,2,0:T(8,128)S(1)}, f32[1,1024,256]{1,2,0:T(8,128)S(1)}, u32[]{:S(2)}, u32[]{:S(2)}) %collective-permute-start) | collective-permute-done | bytes 1048608 | tf_op jit(solution)/shard_map/ppermute | solution.py:14
  271.3 0.2 fusion.102
  271.6 1.2 subtract_convert_fusion.2
  272.8 1.7 fusion.14
  274.5 2.0 fusion.11
  276.5 2.7 fusion.54
  279.3 5.0 %fusion.2 = (f32[4,512]{1,0:T(4,128)S(1)}, f32[1024,512,4]{1,0,2:T(8,128)}) fusion(f32[4,512]{1,0:T(4,128)S(1)} %fusion.11, f32[4,512]{1,0:T(4,128)S(1)} %get-tuple-element.18, f32[1024,512,4]{1,0,2:T(8,128)S(1)} %get-tuple-element.19, pred[512,1024]{0,1:T(8,128)(4,1)S(1)} %iota_compare_fusion, bf16[1,1024,4,128]{1,3,2,0:T(8,128)(2,1)S(1)} %bitcast.210, ...), kind=kOutput, calls=%fused_computation.5 | convolution fusion | flops 549451776 | bytes 18112512 | tf_op jit(solution)/shard_map/sqhd,skd->shqk/dot_general | solution.py:94
  284.3 0.9 fusion.30
  285.2 0.9 fusion.29
  286.1 1.7 fusion.21
  287.8 1.4 fusion.60
  289.2 6.2 %fusion.57 = f32[1,1024,128]{1,2,0:T(8,128)S(1)} fusion(f32[1024,512,4]{1,0,2:T(8,128)} %get-tuple-element.21, f32[4,512]{1,0:T(4,128)S(1)} %get-tuple-element.20, f32[4,512]{1,0:T(4,128)S(1)} %fusion.11, f32[4,512]{1,0:T(4,128)S(1)} %get-tuple-element.18, f32[1024,512,4]{1,0,2:T(8,128)S(1)} %get-tuple-element.19, ...), kind=kOutput, calls=%fused_computation.50 | convolution fusion | flops 554696704 | bytes 18898944 | tf_op jit(solution)/shard_map/shqk,sqhd->skd/dot_general | solution.py:99
  295.4 1.8 fusion.63
  297.4 0.6 collective-permute-start.1
  298.0 23.0 %collective-permute-done.1 = f32[1,1024,256]{1,2,0:T(8,128)S(1)} collective-permute-done((f32[1,1024,256]{1,2,0:T(8,128)S(1)}, f32[1,1024,256]{1,2,0:T(8,128)S(1)}, u32[]{:S(2)}, u32[]{:S(2)}) %collective-permute-start.1) | collective-permute-done | bytes 1048608 | tf_op jit(solution)/shard_map/ppermute | solution.py:14
  321.0 0.2 add.50
  321.3 1.2 add_convert_fusion.1
  322.5 6.0 %fusion.15 = f32[4096,256]{1,0:T(8,128)S(1)} fusion(bf16[1,1024,8192]{2,1,0:T(8,128)(2,1)} %all-gather.2.cloned.1.call-done, s32[]{:T(128)S(6)} %select_n.24, bf16[1024,128]{0,1:T(8,128)(2,1)S(1)} %fusion.75, bf16[1024,128]{0,1:T(8,128)(2,1)S(1)} %maximum_bitcast_fusion.3), kind=kOutput, calls=%fused_computation.19 | convolution fusion | flops 2149580800 | bytes 13107204 | tf_op jit(solution)/shard_map/jyv,jyo->jvo/dot_general | solution.py:116
  328.5 2.2 fusion.103
  330.7 0.7 reduce-scatter.5.cloned.1.call-update
  331.4 8.4 %reduce-scatter.3.cloned.1.call-done = f32[2048,128]{1,0:T(8,128)} async-done(((f32[4096,128]{1,0:T(8,128)}), f32[2048,128]{1,0:T(8,128)}) %reduce-scatter.3.cloned.1.call-update) | async-done | bytes 1048592 | tf_op jit(solution)/shard_map/reduce_scatter | solution.py:121
  339.9 13.7 %reduce-scatter.5.cloned.1.call-done = f32[2048,128]{1,0:T(8,128)} async-done(((f32[4096,128]{1,0:T(8,128)}), f32[2048,128]{1,0:T(8,128)}) %reduce-scatter.5.cloned.1.call-update) | async-done | bytes 1048592 | tf_op jit(solution)/shard_map/reduce_scatter | solution.py:122
  (17 shorter events, 0.6 us)
Async XLA Ops:
  7.2 233.3 %all-gather.2.cloned.1.call-start = ((), (), s32[]{:S(2)}) async-start(), calls=%async_computation.2 | async-start | bytes 18874368 | tf_op jit(solution)/shard_map/all_gather | solution.py:56
  7.9 332.0 %reduce-scatter.3.cloned.1.call-start = ((), (), s32[]{:S(2)}) async-start(), calls=%async_computation.3 | async-start | bytes 3145728 | tf_op jit(solution)/shard_map/reduce_scatter | solution.py:121
  8.0 11.4 %copy-start = (bf16[1,1024,512]{2,1,0:T(8,128)(2,1)S(1)}, bf16[1,1024,512]{2,1,0:T(8,128)(2,1)}, u32[]{:S(2)}) copy-start(bf16[1,1024,512]{2,1,0:T(8,128)(2,1)} %param.10) | copy-start | bytes 3145732
  246.8 24.6 %collective-permute-start = (f32[1,1024,256]{1,2,0:T(8,128)S(1)}, f32[1,1024,256]{1,2,0:T(8,128)S(1)}, u32[]{:S(2)}, u32[]{:S(2)}) collective-permute-start(f32[1,1024,256]{1,2,0:T(8,128)S(1)} %fusion.49), channel_id=1, source_target_pairs={{0,1},{1,0},{2,3},{3,2},{4,5},{5,4},{6,7},{7,6},{8,9},{9,8},{10,11... | collective-permute-start | bytes 3145736 | tf_op jit(solution)/shard_map/ppermute | solution.py:14
  297.4 23.6 %collective-permute-start.1 = (f32[1,1024,256]{1,2,0:T(8,128)S(1)}, f32[1,1024,256]{1,2,0:T(8,128)S(1)}, u32[]{:S(2)}, u32[]{:S(2)}) collective-permute-start(f32[1,1024,256]{1,2,0:T(8,128)S(1)} %fusion.66), channel_id=1, source_target_pairs={{0,1},{1,0},{2,3},{3,2},{4,5},{5,4},{6,7},{7,6},{8,9},{9,8},{10,11... | collective-permute-start | bytes 3145736 | tf_op jit(solution)/shard_map/ppermute | solution.py:14
  330.7 22.9 %reduce-scatter.5.cloned.1.call-start = ((), (), s32[]{:S(2)}) async-start(), calls=%async_computation.4 | async-start | bytes 3145728 | tf_op jit(solution)/shard_map/reduce_scatter | solution.py:122
Sparse Core Ops, SparseCore 0:
  10.1 230.3 all-gather.1
  330.8 9.0 reduce-scatter.2
  342.8 10.7 reduce-scatter.4
where the time goes:
time: 361 us; the launch traced here: 360 us
  waiting for transfers between devices  274 us (76%)
  matrix products  48.1 us (13%)
  between operations  14.6 us (4%)
  local copies, waits for them, and re-layouts  14.2 us (4%)
  other arithmetic  7.71 us (2%)
    all_gather x1, waiting for transfers between devices, local(): collected_rows = lax.all_gather(hidden, 'tensor', axis=1, tiled=True)  218 us
    ppermute x2, waiting for transfers between devices, from_partner(): return lax.ppermute(value, axis, pairs)  32.2 us
    dot_general x1, matrix products, local(): jnp.dot(collected_rows, query_weight, preferred_element_type=jnp.float32)  14.4 us
    reduce_scatter x1, waiting for transfers between devices, local(): lax.psum_scatter(squares[:, head_width:], 'dp', scatter_dimension=0, tile...  13.7 us
    dot_general x1, local copies, waits for them, and re-layouts, local(): jnp.dot(collected_rows, query_weight, preferred_element_type=jnp.float32)  11.4 us
    reduce_scatter x1, waiting for transfers between devices, local(): lax.psum_scatter(squares[:, :head_width], 'dp', scatter_dimension=0, tile...  8.45 us
    dot_general x2, matrix products, local(): jnp.einsum('shqk,sqhd->skd', dscore, query_block, preferred_element_type=...  8.03 us
  transfers between devices with their start and end apart: 5, of which 5 were waited for; matrix products, arithmetic and copies ran while one was open for 8% of the time, Pallas kernels for 0%

commit v1 on v0

--- a/solution.py
+++ b/solution.py
@@ -6,6 +6,24 @@
 
 rope_base = 1000000.0
 far_below = -1e30
+
+
+def ring_gather(shard, axis, dim):
+    ways, here, step = (lax.axis_size(axis), lax.axis_index(axis), shard.shape[dim])
+    shape = [n * ways if d == dim else n for d, n in enumerate(shard.shape)]
+    full = lax.dynamic_update_slice_in_dim(
+        jnp.zeros(shape, shard.dtype), shard, here * step, axis=dim
+    )
+    going_up = going_down = shard
+    for far in range(1, ways // 2 + 1):
+        going_up = lax.ppermute(going_up, axis, [(d, (d + 1) % ways) for d in range(ways)])
+        full = lax.dynamic_update_slice_in_dim(full, going_up, (here - far) % ways * step, axis=dim)
+        if 2 * far < ways:
+            going_down = lax.ppermute(going_down, axis, [(d, (d - 1) % ways) for d in range(ways)])
+            full = lax.dynamic_update_slice_in_dim(
+                full, going_down, (here + far) % ways * step, axis=dim
+            )
+    return full
 
 
 def from_partner(value, axis, stride):
@@ -53,7 +71,7 @@
     score_scale = 1.0 / math.sqrt(head_width)
     angles = angle_table(length, head_width)
     pair_rows = jnp.concatenate([key_weight[0], value_weight[0]], axis=1)
-    collected_rows = lax.all_gather(hidden, "tensor", axis=1, tiled=True)
+    collected_rows = ring_gather(hidden, "tensor", 1)
     query_part = jnp.dot(collected_rows, query_weight, preferred_element_type=jnp.float32)
     own_part = lax.dynamic_slice_in_dim(collected_rows, pair_side * half_width, half_width, 2)
     kv_part = jnp.dot(own_part, pair_rows, preferred_element_type=jnp.float32)

time: 361 us -> 453 us (1.25)
  waiting for transfers between devices: 274 us -> 338 us
  starting transfers between devices: 1.35 us -> 20.3 us
  local copies, waits for them, and re-layouts: 14.2 us -> 23.8 us
    ppermute x0 -> x7, waiting for transfers between devices: none -> 281 us  [the longest x4 236 us: ring_gather(): lax.ppermute(going_up, axis, [(d, (d + 1) % ways) for d in range(ways)])]
    all_gather x1 -> x0, waiting for transfers between devices: 218 us -> none  [local(): collected_rows = lax.all_gather(hidden, 'tensor', axis=1, tiled=True)]
    ppermute x0 -> x7, starting transfers between devices: none -> 19.8 us  [the longest x4 10.4 us: ring_gather(): lax.ppermute(going_up, axis, [(d, (d + 1) % ways) for d in range(ways)])]
    dynamic_update_slice x0 -> x8, local copies, waits for them, and re-layouts: none -> 6.77 us  [the longest x4 4.18 us: ring_gather(): lax.dynamic_update_slice_in_dim(full, going_up, (here - far) % ways * ste...]
  transfers between devices with their start and end apart: 5 -> 11, of which waited for: 5 -> 8; matrix products, arithmetic and copies ran while one was open for 8% -> 8% of each run, Pallas kernels for 0% -> 0%
where the time goes in v1:
time: 453 us; the launch traced here: 452 us
  waiting for transfers between devices  338 us (75%)
  matrix products  44.7 us (10%)
  local copies, waits for them, and re-layouts  23.8 us (5%)
  starting transfers between devices  20.3 us (4%)
  between operations  15.1 us (3%)
  other arithmetic  9.94 us (2%)
    ppermute x4, waiting for transfers between devices, ring_gather(): lax.ppermute(going_up, axis, [(d, (d + 1) % ways) for d in range(ways)])  236 us
    ppermute x3, waiting for transfers between devices, ring_gather(): lax.ppermute(going_down, axis, [(d, (d - 1) % ways) for d in range(ways)])  45.5 us
    ppermute x2, waiting for transfers between devices, from_partner(): return lax.ppermute(value, axis, pairs)  36.3 us
    reduce_scatter x1, waiting for transfers between devices, local(): lax.psum_scatter(squares[:, head_width:], 'dp', scatter_dimension=0, tile...  13.7 us
    dot_general x1, matrix products, local(): jnp.dot(collected_rows, query_weight, preferred_element_type=jnp.float32)  12.5 us
    dot_general x2, matrix products, local(): jnp.einsum('shqk,sqhd->skd', dscore, query_block, preferred_element_type=...  11.7 us
    dot_general x1, local copies, waits for them, and re-layouts, local(): jnp.dot(collected_rows, query_weight, preferred_element_type=jnp.float32)  11.6 us
    ppermute x4, starting transfers between devices, ring_gather(): lax.ppermute(going_up, axis, [(d, (d + 1) % ways) for d in range(ways)])  10.4 us
  transfers between devices with their start and end apart: 11, of which 8 were waited for; matrix products, arithmetic and copies ran while one was open for 8% of the time, Pallas kernels for 0%

profile of v1, /device:TPU:0, one launch (start us, length us, event | category | flops | bytes accessed | tf_op | source)
XLA Modules:
  0.0 451.9 jit_solution(17496174831746953312)
XLA Ops:
  7.2 3.0 collective-permute-start
  10.2 3.1 collective-permute-start.1
  13.3 87.0 %collective-permute-done = bf16[1,128,8192]{2,1,0:T(8,128)(2,1)} collective-permute-done((bf16[1,128,8192]{2,1,0:T(8,128)(2,1)}, bf16[1,128,8192]{2,1,0:T(8,128)(2,1)}, u32[]{:S(2)}, u32[]{:S(2)}) %collective-permute-start) | collective-permute-done | bytes 2097184 | tf_op jit(solution)/shard_map/ppermute | solution.py:19
  100.4 2.5 collective-permute-start.2
  102.9 11.6 %copy.50 = bf16[512,8192]{1,0:T(8,128)(2,1)} copy(bf16[512,8192]{0,1:T(8,128)(2,1)} %bitcast.207) | data formatting | bytes 16777216 | tf_op jit(solution)/shard_map/dot_general | solution.py:75
  117.3 1.6 broadcast_in_dim.34
  119.2 3.2 collective-permute-start.3
  123.4 68.7 %collective-permute-done.2 = bf16[1,128,8192]{2,1,0:T(8,128)(2,1)} collective-permute-done((bf16[1,128,8192]{2,1,0:T(8,128)(2,1)}, bf16[1,128,8192]{2,1,0:T(8,128)(2,1)}, u32[]{:S(2)}, u32[]{:S(2)}) %collective-permute-start.2) | collective-permute-done | bytes 2097184 | tf_op jit(solution)/shard_map/ppermute | solution.py:19
  192.1 2.5 collective-permute-start.4
  194.6 1.8 constant_dynamic-update-slice_fusion.6
  196.5 1.8 constant_dynamic-update-slice_fusion.5
  198.3 3.1 collective-permute-start.5
  201.4 1.8 constant_dynamic-update-slice_fusion.4
  203.3 79.9 %collective-permute-done.4 = bf16[1,128,8192]{2,1,0:T(8,128)(2,1)S(1)} collective-permute-done((bf16[1,128,8192]{2,1,0:T(8,128)(2,1)}, bf16[1,128,8192]{2,1,0:T(8,128)(2,1)S(1)}, u32[]{:S(2)}, u32[]{:S(2)}) %collective-permute-start.4) | collective-permute-done | bytes 2097184 | tf_op jit(solution)/shard_map/ppermute | solution.py:19
  283.2 2.4 collective-permute-start.6
  286.1 45.5 %collective-permute-done.5 = bf16[1,128,8192]{2,1,0:T(8,128)(2,1)S(1)} collective-permute-done((bf16[1,128,8192]{2,1,0:T(8,128)(2,1)S(1)}, bf16[1,128,8192]{2,1,0:T(8,128)(2,1)S(1)}, u32[]{:S(2)}, u32[]{:S(2)}) %collective-permute-start.5) | collective-permute-done | bytes 2097184 | tf_op jit(solution)/shard_map/ppermute | solution.py:22
  332.8 2.4 fusion.49
  335.3 12.5 %fusion.44 = f32[1,1024,4,128]{1,3,2,0:T(8,128)S(1)} fusion(bf16[4,128,8192]{2,1,0:T(8,128)(2,1)} %bitcast.208, bf16[1,1024,8192]{2,1,0:T(8,128)(2,1)S(1)} %constant_dynamic-update-slice_fusion), kind=kOutput, calls=%fused_computation.47 | convolution fusion | flops 8589934592 | bytes 27262976 | tf_op jit(solution)/shard_map/dot_general | solution.py:75
  348.1 12.3 %collective-permute-done.7 = f32[1,1024,256]{1,2,0:T(8,128)} collective-permute-done((f32[1,1024,256]{1,2,0:T(8,128)S(1)}, f32[1,1024,256]{1,2,0:T(8,128)}, u32[]{:S(2)}, u32[]{:S(2)}) %collective-permute-start.7) | collective-permute-done | bytes 1048608 | tf_op jit(solution)/shard_map/ppermute | solution.py:32
  363.1 1.7 fusion.14
  364.8 1.8 fusion.11
  366.8 2.7 fusion.54
  369.6 5.2 %fusion.2 = (f32[4,512]{1,0:T(4,128)S(1)}, f32[1024,512,4]{1,0,2:T(8,128)}) fusion(f32[4,512]{1,0:T(4,128)S(1)} %fusion.11, f32[4,512]{1,0:T(4,128)S(1)} %get-tuple-element.18, f32[1024,512,4]{1,0,2:T(8,128)S(1)} %get-tuple-element.19, pred[512,1024]{0,1:T(8,128)(4,1)S(1)} %iota_compare_fusion, bf16[1,1024,4,128]{1,3,2,0:T(8,128)(2,1)S(1)} %bitcast.210, ...), kind=kOutput, calls=%fused_computation.5 | convolution fusion | flops 549451776 | bytes 18112512 | tf_op jit(solution)/shard_map/sqhd,skd->shqk/dot_general | solution.py:112
  376.6 3.5 fusion.21
  381.5 7.7 %fusion.57 = f32[1,1024,128]{1,2,0:T(8,128)S(1)} fusion(f32[1024,512,4]{1,0,2:T(8,128)} %get-tuple-element.21, f32[4,512]{1,0:T(4,128)S(1)} %get-tuple-element.20, f32[4,512]{1,0:T(4,128)S(1)} %fusion.11, f32[4,512]{1,0:T(4,128)S(1)} %get-tuple-element.18, f32[1024,512,4]{1,0,2:T(8,128)} %copy-done, pred[512,1024]{0,1:T(8,128)(4,1)S(1)} %iota_compare_fusion, ...), kind=kOutput, calls=%fused_computation.50 | convolution fusion | flops 554696704 | bytes 18898944 | tf_op jit(solution)/shard_map/shqk,sqhd->skd/dot_general | solution.py:117
  389.2 4.1 fusion.63
  393.7 24.0 %collective-permute-done.8 = f32[1,1024,256]{1,2,0:T(8,128)S(1)} collective-permute-done((f32[1,1024,256]{1,2,0:T(8,128)S(1)}, f32[1,1024,256]{1,2,0:T(8,128)S(1)}, u32[]{:S(2)}, u32[]{:S(2)}) %collective-permute-start.8) | collective-permute-done | bytes 1048608 | tf_op jit(solution)/shard_map/ppermute | solution.py:32
  417.9 1.4 add_convert_fusion.1
  419.4 2.7 fusion.15
  422.1 2.2 fusion.103
  425.1 6.3 %reduce-scatter.3.cloned.1.call-done = f32[2048,128]{1,0:T(8,128)} async-done(((f32[4096,128]{1,0:T(8,128)}), f32[2048,128]{1,0:T(8,128)}) %reduce-scatter.3.cloned.1.call-update) | async-done | bytes 1048592 | tf_op jit(solution)/shard_map/reduce_scatter | solution.py:139
  431.4 13.7 %reduce-scatter.5.cloned.1.call-done = f32[2048,128]{1,0:T(8,128)} async-done(((f32[4096,128]{1,0:T(8,128)}), f32[2048,128]{1,0:T(8,128)}) %reduce-scatter.5.cloned.1.call-update) | async-done | bytes 1048592 | tf_op jit(solution)/shard_map/reduce_scatter | solution.py:140
  (47 shorter events, 13.0 us)
Async XLA Ops:
  7.2 424.2 %reduce-scatter.3.cloned.1.call-start = ((), (), s32[]{:S(2)}) async-start(), calls=%async_computation.2 | async-start | bytes 3145728 | tf_op jit(solution)/shard_map/reduce_scatter | solution.py:139
  7.2 93.2 %collective-permute-start = (bf16[1,128,8192]{2,1,0:T(8,128)(2,1)}, bf16[1,128,8192]{2,1,0:T(8,128)(2,1)}, u32[]{:S(2)}, u32[]{:S(2)}) collective-permute-start(bf16[1,128,8192]{2,1,0:T(8,128)(2,1)} %param.6), channel_id=1, source_target_pairs={{0,1},{1,2},{2,3},{3,4},{4,5},{5,6},{6,7},{7,0},{8,9},{9,10},{10,1... | collective-permute-start | bytes 6291464 | tf_op jit(solution)/shard_map/ppermute | solution.py:19
  10.2 109.0 %collective-permute-start.1 = (bf16[1,128,8192]{2,1,0:T(8,128)(2,1)}, bf16[1,128,8192]{2,1,0:T(8,128)(2,1)}, u32[]{:S(2)}, u32[]{:S(2)}) collective-permute-start(bf16[1,128,8192]{2,1,0:T(8,128)(2,1)} %param.6), channel_id=1, source_target_pairs={{0,7},{1,0},{2,1},{3,2},{4,3},{5,4},{6,5},{7,6},{8,15},{9,8},{10,9... | collective-permute-start | bytes 6291464 | tf_op jit(solution)/shard_map/ppermute | solution.py:22
  100.4 91.8 %collective-permute-start.2 = (bf16[1,128,8192]{2,1,0:T(8,128)(2,1)}, bf16[1,128,8192]{2,1,0:T(8,128)(2,1)}, u32[]{:S(2)}, u32[]{:S(2)}) collective-permute-start(bf16[1,128,8192]{2,1,0:T(8,128)(2,1)} %collective-permute-done), channel_id=1, source_target_pairs={{0,1},{1,2},{2,3},{3,4},{4,5},{5,6},{6,7},{7,0},{8,9},{9,10},{10,1... | collective-permute-start | bytes 6291464 | tf_op jit(solution)/shard_map/ppermute | solution.py:19
  102.9 11.6 %copy-start.2 = (bf16[1,1024,512]{2,1,0:T(8,128)(2,1)S(1)}, bf16[1,1024,512]{2,1,0:T(8,128)(2,1)}, u32[]{:S(2)}) copy-start(bf16[1,1024,512]{2,1,0:T(8,128)(2,1)} %param.10) | copy-start | bytes 3145732
  117.3 1.7 copy-start.1
  119.2 79.1 %collective-permute-start.3 = (bf16[1,128,8192]{2,1,0:T(8,128)(2,1)}, bf16[1,128,8192]{2,1,0:T(8,128)(2,1)S(1)}, u32[]{:S(2)}, u32[]{:S(2)}) collective-permute-start(bf16[1,128,8192]{2,1,0:T(8,128)(2,1)} %collective-permute-done.1), channel_id=1, source_target_pairs={{0,7},{1,0},{2,1},{3,2},{4,3},{5,4},{6,5},{7,6},{8,15},{9,8},{10,9... | collective-permute-start | bytes 6291464 | tf_op jit(solution)/shard_map/ppermute | solution.py:22
  192.1 91.1 %collective-permute-start.4 = (bf16[1,128,8192]{2,1,0:T(8,128)(2,1)}, bf16[1,128,8192]{2,1,0:T(8,128)(2,1)S(1)}, u32[]{:S(2)}, u32[]{:S(2)}) collective-permute-start(bf16[1,128,8192]{2,1,0:T(8,128)(2,1)} %collective-permute-done.2), channel_id=1, source_target_pairs={{0,1},{1,2},{2,3},{3,4},{4,5},{5,6},{6,7},{7,0},{8,9},{9,10},{10,1... | collective-permute-start | bytes 6291464 | tf_op jit(solution)/shard_map/ppermute | solution.py:19
  198.3 133.2 %collective-permute-start.5 = (bf16[1,128,8192]{2,1,0:T(8,128)(2,1)S(1)}, bf16[1,128,8192]{2,1,0:T(8,128)(2,1)S(1)}, u32[]{:S(2)}, u32[]{:S(2)}) collective-permute-start(bf16[1,128,8192]{2,1,0:T(8,128)(2,1)S(1)} %collective-permute-done.3), channel_id=1, source_target_pairs={{0,7},{1,0},{2,1},{3,2},{4,3},{5,4},{6,5},{7,6},{8,15},{9,8},{10,9... | collective-permute-start | bytes 6291464 | tf_op jit(solution)/shard_map/ppermute | solution.py:22
  283.2 48.6 %collective-permute-start.6 = (bf16[1,128,8192]{2,1,0:T(8,128)(2,1)S(1)}, bf16[1,128,8192]{2,1,0:T(8,128)(2,1)S(1)}, u32[]{:S(2)}, u32[]{:S(2)}) collective-permute-start(bf16[1,128,8192]{2,1,0:T(8,128)(2,1)S(1)} %collective-permute-done.4), channel_id=1, source_target_pairs={{0,1},{1,2},{2,3},{3,4},{4,5},{5,6},{6,7},{7,0},{8,9},{9,10},{10,1... | collective-permute-start | bytes 6291464 | tf_op jit(solution)/shard_map/ppermute | solution.py:19
  286.1 46.0 %copy-start.4 = (bf16[1,4096,128]{2,1,0:T(8,128)(2,1)S(1)}, bf16[1,4096,128]{2,1,0:T(8,128)(2,1)}, u32[]{:S(2)}) copy-start(bf16[1,4096,128]{2,1,0:T(8,128)(2,1)} %param.9) | copy-start | bytes 3145732
  331.6 1.2 copy-start.5
  335.2 25.3 %collective-permute-start.7 = (f32[1,1024,256]{1,2,0:T(8,128)S(1)}, f32[1,1024,256]{1,2,0:T(8,128)}, u32[]{:S(2)}, u32[]{:S(2)}) collective-permute-start(f32[1,1024,256]{1,2,0:T(8,128)S(1)} %fusion.49), channel_id=1, source_target_pairs={{0,1},{1,0},{2,3},{3,2},{4,5},{5,4},{6,7},{7,6},{8,9},{9,8},{10,11... | collective-permute-start | bytes 3145736 | tf_op jit(solution)/shard_map/ppermute | solution.py:32
  364.8 4.8 %copy-start = (f32[1024,512,4]{1,0,2:T(8,128)}, f32[1024,512,4]{1,0,2:T(8,128)S(1)}, u32[]{:S(2)}) copy-start(f32[1024,512,4]{1,0,2:T(8,128)S(1)} %get-tuple-element.19) | copy-start | bytes 25165828
  364.8 2.0 copy-start.3
  393.4 24.3 %collective-permute-start.8 = (f32[1,1024,256]{1,2,0:T(8,128)S(1)}, f32[1,1024,256]{1,2,0:T(8,128)S(1)}, u32[]{:S(2)}, u32[]{:S(2)}) collective-permute-start(f32[1,1024,256]{1,2,0:T(8,128)S(1)} %fusion.66), channel_id=1, source_target_pairs={{0,1},{1,0},{2,3},{3,2},{4,5},{5,4},{6,7},{7,6},{8,9},{9,8},{10,11... | collective-permute-start | bytes 3145736 | tf_op jit(solution)/shard_map/ppermute | solution.py:32
  424.3 20.8 %reduce-scatter.5.cloned.1.call-start = ((), (), s32[]{:S(2)}) async-start(), calls=%async_computation.3 | async-start | bytes 3145728 | tf_op jit(solution)/shard_map/reduce_scatter | solution.py:140
Sparse Core Ops, SparseCore 0:
  424.4 6.8 reduce-scatter.2
  434.3 10.7 reduce-scatter.4
